TPU v7x, 32 devices: a whole 2x2x4 slice. The times are simulated.
32 devices in a mesh: row: 4 (over y, core), col: 8 (over z, x).
Axes of the slice: x: 2, y: 2, z: 4, core: 2. Of those that a mesh axis runs over, the one named last changes fastest.
Arguments:
- left: bfloat16 [128, 8192], P('col', 'row'), may hold values from -6 to 6
- right: bfloat16 [128, 8192], P('row', 'col'), may hold values from -6 to 6
- proj: bfloat16 [1024, 128], replicated, may hold values from -2 to 2
- bias: float32 [128], replicated, may hold values from -1 to 1
- pair_grad: bfloat16 [256, 256, 128], P('row', 'col'), may hold values from -0.1875 to 0.1875
Outputs:
- pair_out: bfloat16 [256, 256, 128], P('row', 'col')
- left_grad: float32 [128, 8192], P('col', 'row')
- right_grad: float32 [128, 8192], P('row', 'col')
- proj_grad: float32 [1024, 128], replicated
All inputs are finite; a program needn't handle non-finite values.
Results may differ from a plain program's by a relative error of at most 0.0056.
Values may be sent and summed in bfloat16 or wider, within the bound.
A program may use at most 128 MiB of HBM per device.

v0:
```python
import jax
import jax.numpy as jnp
from jax import lax
from jax.sharding import PartitionSpec as P

CH = 32
PAIR = 128
SEQS = 128
OUTER = 1024


def shards(left, right, proj, bias, pair_grad):
    left_all = lax.all_gather(left, "col", axis=0, tiled=True)
    right_all = lax.all_gather(right, "row", axis=0, tiled=True)
    seq_count = left_all.shape[0]
    rows_here = left_all.shape[1] // CH
    cols_here = right_all.shape[1] // CH
    left_cube = left_all.reshape(seq_count, rows_here, CH)
    right_cube = right_all.reshape(seq_count, cols_here, CH)
    square = (
        jnp.einsum("sic,sje->ijce", left_cube, right_cube, preferred_element_type=jnp.float32)
        / SEQS
    )
    outers = square.astype(jnp.bfloat16).reshape(rows_here * cols_here, OUTER)
    preact = jnp.dot(outers, proj, preferred_element_type=jnp.float32) + bias
    active = jnp.maximum(preact, 0.0)
    pair_out = (active * active).astype(jnp.bfloat16).reshape(rows_here, cols_here, PAIR)
    grad_pre = (
        pair_grad.reshape(rows_here * cols_here, PAIR).astype(jnp.float32) * 2.0 * active
    ).astype(jnp.bfloat16)
    weight_term = lax.dot_general(
        outers, grad_pre, (((0,), (0,)), ((), ())), preferred_element_type=jnp.float32
    )
    proj_grad = lax.psum(weight_term, ("row", "col"))
    grad_outer = jnp.dot(grad_pre, proj.T, preferred_element_type=jnp.float32).astype(jnp.bfloat16)
    grad_cube = grad_outer.reshape(rows_here, cols_here, CH, CH)
    left_whole = (
        jnp.einsum("ijce,sje->sic", grad_cube, right_cube, preferred_element_type=jnp.float32)
        / SEQS
    )
    right_whole = (
        jnp.einsum("ijce,sic->sje", grad_cube, left_cube, preferred_element_type=jnp.float32) / SEQS
    )
    left_grad = lax.psum_scatter(
        left_whole.reshape(seq_count, rows_here * CH), "col", scatter_dimension=0, tiled=True
    )
    right_grad = lax.psum_scatter(
        right_whole.reshape(seq_count, cols_here * CH), "row", scatter_dimension=0, tiled=True
    )
    return (pair_out, left_grad, right_grad, proj_grad)


def solution(mesh):
    return jax.shard_map(
        shards,
        mesh=mesh,
        in_specs=(P("col", "row"), P("row", "col"), P(), P(), P("row", "col", None)),
        out_specs=(P("row", "col", None), P("col", "row"), P("row", "col"), P()),
        check_vma=False,
    )
```

profile of v0, /device:TPU:0, one launch (start us, length us, event | category | flops | bytes accessed | tf_op | source)
XLA Modules:
  0.0 248.4 jit_solution(3948851120335303654)
XLA Ops:
  8.0 0.0 copy-start
  8.0 0.0 all-reduce.2.cloned.1.call-start
  8.1 33.4 %all_gather.7 = bf16[128,2048]{1,0:T(8,128)(2,1)S(1)} all-gather(bf16[16,2048]{1,0:T(8,128)(2,1)} %param.5), channel_id=1, replica_groups=mesh['row'=4,'col'=8] {'col'}, dimensions={0}, use_global_device_ids=true | all-gather | bytes 589824 | tf_op jit(solution)/shard_map/all_gather | solution.py:13
  41.4 0.3 copy.26
  41.7 6.0 %all_gather.6 = bf16[128,1024]{1,0:T(8,128)(2,1)S(1)} all-gather(bf16[32,1024]{1,0:T(8,128)(2,1)} %param.6), channel_id=1, replica_groups=mesh['row'=4,'col'=8] {'row'}, dimensions={0}, use_global_device_ids=true | all-gather | bytes 327680 | tf_op jit(solution)/shard_map/all_gather | solution.py:14
  47.7 0.2 copy.25
  47.9 5.6 %fusion = bf16[64,32,32,32]{0,3,2,1:T(8,128)(2,1)} fusion(bf16[128,32,32,1]{0,2,3,1:T(8,128)(2,1)S(1)} %bitcast.50, bf16[128,64,32]{0,2,1:T(8,128)(2,1)S(1)} %bitcast.48), kind=kOutput, calls=%fused_computation.1 | convolution fusion | flops 541065216 | bytes 4980736 | tf_op jit(solution)/shard_map/sic,sje->ijce/dot_general | solution.py:21
  53.5 24.6 %copy.28 = bf16[64,32,32,32]{3,2,1,0:T(8,128)(2,1)} copy(bf16[64,32,32,32]{0,3,2,1:T(8,128)(2,1)} %fusion) | data formatting | bytes 8388608 | tf_op jit(solution)/shard_map/convert_element_type | solution.py:24
  78.1 0.0 copy-start.2
  78.1 0.0 copy-start.3
  78.1 23.3 %reshape.36 = bf16[2048,1024]{1,0:T(8,128)(2,1)} reshape(bf16[64,32,32,32]{3,2,1,0:T(8,128)(2,1)} %copy.28) | data formatting | bytes 8388608 | tf_op jit(solution)/shard_map/reshape | solution.py:24
  101.4 0.0 copy-done.2
  101.4 0.0 copy-start.1
  101.4 0.1 convert_multiply_fusion
  101.6 0.0 copy-done
  101.6 0.0 copy-done.3
  101.6 4.4 %fusion.4 = (bf16[2048,128]{1,0:T(8,128)(2,1)S(1)}, bf16[2048,128]{1,0:T(8,128)(2,1)}) fusion(f32[64,32,128]{2,1,0:T(8,128)S(1)} %convert_multiply_fusion, f32[128]{0:T(128)S(1)} %copy-done.3, bf16[2048,1024]{1,0:T(8,128)(2,1)} %reshape.36, bf16[1024,128]{1,0:T(8,128)(2,1)S(1)} %copy-done), kind=kOutput, calls=%fused_computation.10 | convolution fusion | flops 538443776 | bytes 6554112 | tf_op jit(solution)/shard_map/dot_general | solution.py:25
  106.0 0.0 copy-done.1
  106.0 2.1 fusion.7
  108.1 0.0 all-reduce.2.cloned.1.call-update
  108.1 0.2 reduce-scatter.5.cloned.1.call-start
  108.3 3.2 %convolution_convert_fusion = bf16[2048,1024]{1,0:T(8,128)(2,1)} fusion(bf16[2048,128]{1,0:T(8,128)(2,1)S(1)} %get-tuple-element.4, bf16[1024,128]{1,0:T(8,128)(2,1)S(1)} %copy-done), kind=kOutput, calls=%fused_computation.2 | convolution fusion | flops 538968064 | bytes 4980736 | tf_op jit(solution)/shard_map/dot_general | solution.py:35
  111.5 20.3 %reshape.38 = bf16[64,32,32,32]{3,2,1,0:T(8,128)(2,1)} reshape(bf16[2048,1024]{1,0:T(8,128)(2,1)} %convolution_convert_fusion) | data formatting | bytes 8388608 | tf_op jit(solution)/shard_map/reshape | solution.py:36
  131.9 10.3 %fusion.3 = f32[32,32,128]{2,1,0:T(8,128)S(1)} fusion(bf16[64,32,32,32]{3,2,1,0:T(8,128)(2,1)} %reshape.38, bf16[128,64,32,1]{0,2,3,1:T(8,128)(2,1)S(1)} %bitcast.49), kind=kOutput, calls=%fused_computation.8 | convolution fusion | flops 537001984 | bytes 5242880 | tf_op jit(solution)/shard_map/ijce,sic->sje/dot_general | solution.py:42
  142.2 1.0 copy.31
  143.2 0.0 reduce-scatter.5.cloned.1.call-update
  143.2 0.0 reduce-scatter.3.cloned.1.call-start
  143.3 9.1 %fusion.2 = f32[64,32,128]{2,1,0:T(8,128)S(1)} fusion(bf16[64,32,32,32]{3,2,1,0:T(8,128)(2,1)} %reshape.38, bf16[128,32,32,1]{0,2,1,3:T(8,128)(2,1)S(1)} %bitcast.51), kind=kOutput, calls=%fused_computation.6 | convolution fusion | flops 537133056 | bytes 5505024 | tf_op jit(solution)/shard_map/ijce,sje->sic/dot_general | solution.py:38
  152.4 1.3 copy.29
  153.7 0.0 reduce-scatter.3.cloned.1.call-update
  153.8 85.4 %all-reduce.2.cloned.1.call-done = f32[1024,128]{1,0:T(8,128)} async-done(((f32[1024,128]{1,0:T(8,128)}), f32[1024,128]{1,0:T(8,128)}) %all-reduce.2.cloned.1.call-update) | async-done | bytes 524304 | tf_op jit(solution)/shard_map/psum | solution.py:34
  239.1 1.9 copy.41
  (2 shorter events, 0.0 us)
Async XLA Ops:
  8.0 93.6 %copy-start = (bf16[1024,128]{1,0:T(8,128)(2,1)S(1)}, bf16[1024,128]{1,0:T(8,128)(2,1)}, u32[]{:S(2)}) copy-start(bf16[1024,128]{1,0:T(8,128)(2,1)} %param.7) | copy-start | bytes 786436
  8.0 231.1 %all-reduce.2.cloned.1.call-start = ((), (), s32[]{:S(2)}) async-start(), calls=%async_computation.4 | async-start | bytes 1048576 | tf_op jit(solution)/shard_map/psum | solution.py:34
  78.1 23.3 %copy-start.2 = (bf16[64,32,128]{2,1,0:T(8,128)(2,1)S(1)}, bf16[64,32,128]{2,1,0:T(8,128)(2,1)}, u32[]{:S(2)}) copy-start(bf16[64,32,128]{2,1,0:T(8,128)(2,1)} %param.9) | copy-start | bytes 1572868
  78.1 23.5 %copy-start.3 = (f32[128]{0:T(128)S(1)}, f32[128]{0:T(128)}, u32[]{:S(2)}) copy-start(f32[128]{0:T(128)} %param.8) | copy-start | bytes 1540
  101.4 4.5 %copy-start.1 = (bf16[2048,1024]{1,0:T(8,128)(2,1)S(1)}, bf16[2048,1024]{1,0:T(8,128)(2,1)}, u32[]{:S(2)}) copy-start(bf16[2048,1024]{1,0:T(8,128)(2,1)} %reshape.36) | copy-start | bytes 12582916
  108.1 131.0 %reduce-scatter.5.cloned.1.call-start = ((), (), s32[]{:S(2)}) async-start(), calls=%async_computation.3 | async-start | bytes 655360 | tf_op jit(solution)/shard_map/reduce_scatter | solution.py:47
  143.2 95.9 %reduce-scatter.3.cloned.1.call-start = ((), (), s32[]{:S(2)}) async-start(), calls=%async_computation.2 | async-start | bytes 1179648 | tf_op jit(solution)/shard_map/reduce_scatter | solution.py:44
Sparse Core Ops, SparseCore 0:
  108.2 130.8 all-reduce.1
Sparse Core Ops, SparseCore 1:
  143.3 22.7 reduce-scatter.4
  169.9 64.3 reduce-scatter.2
where the time goes:
time: 250 us; the launch traced here: 248 us
  waiting for transfers between devices  85.4 us (34%)
  local copies, waits for them, and re-layouts  72.9 us (29%)
  blocking collectives  39.4 us (16%)
  matrix products  34.8 us (14%)
  between operations  15.5 us (6%)
    psum x1, waiting for transfers between devices, shards(): proj_grad = lax.psum(weight_term, ('row', 'col'))  85.4 us
    all_gather x1, blocking collectives, shards(): left_all = lax.all_gather(left, 'col', axis=0, tiled=True)  33.4 us
    convert_element_type x1, local copies, waits for them, and re-layouts, shards(): outers = square.astype(jnp.bfloat16).reshape(rows_here * cols_here, OUTER)  24.6 us
    reshape x1, local copies, waits for them, and re-layouts, shards(): outers = square.astype(jnp.bfloat16).reshape(rows_here * cols_here, OUTER)  23.3 us
    reshape x1, local copies, waits for them, and re-layouts, shards(): grad_cube = grad_outer.reshape(rows_here, cols_here, CH, CH)  20.3 us
    dot_general x1, matrix products, shards(): jnp.einsum('ijce,sic->sje', grad_cube, left_cube, preferred_element_type=...  10.3 us
    dot_general x1, matrix products, shards(): jnp.einsum('ijce,sje->sic', grad_cube, right_cube, preferred_element_type...  9.14 us
    all_gather x1, blocking collectives, shards(): right_all = lax.all_gather(right, 'row', axis=0, tiled=True)  5.99 us
  transfers between devices with their start and end apart: 3, of which 1 were waited for; matrix products, arithmetic and copies ran while one was open for 18% of the time, Pallas kernels for 0%

commit v1 on v0

--- a/solution.py
+++ b/solution.py
@@ -9,8 +9,31 @@
 OUTER = 1024
 
 
+def joined_along(pieces, dim):
+    pieces = jnp.moveaxis(pieces, 0, dim)
+    dims = pieces.shape
+    return pieces.reshape(*dims[:dim], dims[dim] * dims[dim + 1], *dims[dim + 2 :])
+
+
+def grow_blocks(x, axis):
+    devices, index = (lax.axis_size(axis), lax.axis_index(axis))
+    blocks, stride = (x[None], 1)
+    while stride < devices:
+        received = lax.ppermute(blocks, axis, [(i, i ^ stride) for i in range(devices)])
+        low = index & stride == 0
+        blocks = jnp.concatenate(
+            [jnp.where(low, blocks, received), jnp.where(low, received, blocks)]
+        )
+        stride *= 2
+    return blocks
+
+
+def doubled_up(shard, axis, dim):
+    return joined_along(grow_blocks(shard, axis), dim)
+
+
 def shards(left, right, proj, bias, pair_grad):
-    left_all = lax.all_gather(left, "col", axis=0, tiled=True)
+    left_all = doubled_up(left, "col", 0)
     right_all = lax.all_gather(right, "row", axis=0, tiled=True)
     seq_count = left_all.shape[0]
     rows_here = left_all.shape[1] // CH

time: 250 us -> 230 us (0.920)
  blocking collectives: 39.4 us -> 5.97 us
  local copies, waits for them, and re-layouts: 72.9 us -> 49.6 us
  waiting for transfers between devices: 85.4 us -> 99.7 us
  matrix products: 34.8 us -> 46.5 us
  starting transfers between devices: 0.31 us -> 8.2 us
  other arithmetic: 0.12 us -> 3.15 us
    all_gather x1 -> x0, blocking collectives: 33.4 us -> none  [shards(): left_all = lax.all_gather(left, 'col', axis=0, tiled=True)]
    convert_element_type x1 -> x0, local copies, waits for them, and re-layouts: 24.6 us -> none  [shards(): outers = square.astype(jnp.bfloat16).reshape(rows_here * cols_here, OUTER)]
    ppermute x0 -> x3, waiting for transfers between devices: none -> 12.7 us  [grow_blocks(): lax.ppermute(blocks, axis, [(i, i ^ stride) for i in range(devices)])]
    dot_general x1, matrix products: 5.64 us -> 16.2 us  [shards(): jnp.einsum('sic,sje->ijce', left_cube, right_cube, preferred_element_type...]
    ppermute x0 -> x3, starting transfers between devices: none -> 7.86 us  [grow_blocks(): lax.ppermute(blocks, axis, [(i, i ^ stride) for i in range(devices)])]
  transfers between devices with their start and end apart: 3 -> 6, of which waited for: 1 -> 3; matrix products, arithmetic and copies ran while one was open for 18% -> 20% of each run, Pallas kernels for 0% -> 0%
where the time goes in v1:
time: 230 us; the launch traced here: 229 us
  waiting for transfers between devices  99.7 us (43%)
  local copies, waits for them, and re-layouts  49.6 us (22%)
  matrix products  46.5 us (20%)
  between operations  15.6 us (7%)
  starting transfers between devices  8.2 us (4%)
  blocking collectives  5.97 us (3%)
  other arithmetic  3.15 us (1%)
    psum x1, waiting for transfers between devices, shards(): proj_grad = lax.psum(weight_term, ('row', 'col'))  87 us
    reshape x1, local copies, waits for them, and re-layouts, shards(): outers = square.astype(jnp.bfloat16).reshape(rows_here * cols_here, OUTER)  23.3 us
    reshape x1, local copies, waits for them, and re-layouts, shards(): grad_cube = grad_outer.reshape(rows_here, cols_here, CH, CH)  20.3 us
    dot_general x1, matrix products, shards(): jnp.einsum('sic,sje->ijce', left_cube, right_cube, preferred_element_type...  16.2 us
    ppermute x3, waiting for transfers between devices, grow_blocks(): lax.ppermute(blocks, axis, [(i, i ^ stride) for i in range(devices)])  12.7 us
    dot_general x1, matrix products, shards(): jnp.einsum('ijce,sic->sje', grad_cube, left_cube, preferred_element_type=...  11 us
    dot_general x1, matrix products, shards(): jnp.einsum('ijce,sje->sic', grad_cube, right_cube, preferred_element_type...  9.24 us
    ppermute x3, starting transfers between devices, grow_blocks(): lax.ppermute(blocks, axis, [(i, i ^ stride) for i in range(devices)])  7.86 us
  transfers between devices with their start and end apart: 6, of which 3 were waited for; matrix products, arithmetic and copies ran while one was open for 20% of the time, Pallas kernels for 0%

profile of v1, /device:TPU:0, one launch (start us, length us, event | category | flops | bytes accessed | tf_op | source)
XLA Modules:
  0.0 228.7 jit_solution(169458722630119557)
XLA Ops:
  8.0 0.0 copy-start
  8.0 0.0 all-reduce.2.cloned.1.call-start
  8.1 3.0 %collective-permute-start = (bf16[1,16,2048]{2,1,0:T(8,128)(2,1)}, bf16[1,16,2048]{2,1,0:T(8,128)(2,1)S(1)}, u32[]{:S(2)}, u32[]{:S(2)}) collective-permute-start(bf16[1,16,2048]{2,1,0:T(8,128)(2,1)} %bitcast.48), channel_id=1, source_target_pairs={{0,1},{1,0},{2,3},{3,2},{4,5},{5,4},{6,7},{7,6},{8,9},{9,8},{10,11... | collective-permute-start | bytes 196616 | tf_op jit(solution)/shard_map/ppermute | solution.py:22
  11.1 2.5 %collective-permute-done = bf16[1,16,2048]{2,1,0:T(8,128)(2,1)S(1)} collective-permute-done((bf16[1,16,2048]{2,1,0:T(8,128)(2,1)}, bf16[1,16,2048]{2,1,0:T(8,128)(2,1)S(1)}, u32[]{:S(2)}, u32[]{:S(2)}) %collective-permute-start) | collective-permute-done | bytes 65568 | tf_op jit(solution)/shard_map/ppermute | solution.py:22
  13.5 0.9 broadcast_select_fusion.5
  14.4 2.2 collective-permute-start.1
  16.6 6.0 %all_gather.3 = bf16[128,1024]{1,0:T(8,128)(2,1)S(1)} all-gather(bf16[32,1024]{1,0:T(8,128)(2,1)} %param.6), channel_id=1, replica_groups=mesh['row'=4,'col'=8] {'row'}, dimensions={0}, use_global_device_ids=true | all-gather | bytes 327680 | tf_op jit(solution)/shard_map/all_gather | solution.py:37
  22.6 0.2 copy.17
  22.7 0.0 collective-permute-done.1
  22.8 2.7 %collective-permute-start.2 = (bf16[4,16,2048]{2,1,0:T(8,128)(2,1)S(1)}, bf16[4,16,2048]{2,1,0:T(8,128)(2,1)S(1)}, u32[]{:S(2)}, u32[]{:S(2)}) collective-permute-start(bf16[4,16,2048]{2,1,0:T(8,128)(2,1)S(1)} %pad_maximum_fusion.1), channel_id=1, source_target_pairs={{0,4},{1,5},{2,6},{3,7},{4,0},{5,1},{6,2},{7,3},{8,12},{9,13},{10,... | collective-permute-start | bytes 786440 | tf_op jit(solution)/shard_map/ppermute | solution.py:22
  25.5 2.1 convert_multiply_fusion
  27.6 10.2 %collective-permute-done.2 = bf16[4,16,2048]{2,1,0:T(8,128)(2,1)S(1)} collective-permute-done((bf16[4,16,2048]{2,1,0:T(8,128)(2,1)S(1)}, bf16[4,16,2048]{2,1,0:T(8,128)(2,1)S(1)}, u32[]{:S(2)}, u32[]{:S(2)}) %collective-permute-start.2) | collective-permute-done | bytes 262176 | tf_op jit(solution)/shard_map/ppermute | solution.py:22
  37.9 1.6 reshape_reshape.3
  39.6 16.2 %fusion = bf16[64,32,32,32]{3,2,1,0:T(8,128)(2,1)} fusion(bf16[128,32,32,1]{0,2,1,3:T(8,128)(2,1)S(1)} %bitcast.43, bf16[128,64,32,1]{2,1,0,3:T(8,128)(2,1)S(1)} %bitcast.41), kind=kOutput, calls=%fused_computation.1 | convolution fusion | flops 541065216 | bytes 4980736 | tf_op jit(solution)/shard_map/sic,sje->ijce/dot_general | solution.py:44
  55.8 23.3 %reshape.32 = bf16[2048,1024]{1,0:T(8,128)(2,1)} reshape(bf16[64,32,32,32]{3,2,1,0:T(8,128)(2,1)} %fusion) | data formatting | bytes 8388608 | tf_op jit(solution)/shard_map/reshape | solution.py:47
  79.1 0.0 copy-done
  79.1 0.0 copy-done.2
  79.1 4.7 %fusion.17 = (bf16[2048,128]{1,0:T(8,128)(2,1)S(1)}, bf16[2048,128]{1,0:T(8,128)(2,1)}) fusion(f32[64,32,128]{2,1,0:T(8,128)} %convert_multiply_fusion, f32[128]{0:T(128)S(1)} %copy-done.2, bf16[2048,1024]{1,0:T(8,128)(2,1)} %reshape.32, bf16[1024,128]{1,0:T(8,128)(2,1)S(1)} %copy-done), kind=kOutput, calls=%fused_computation.14 | convolution fusion | flops 538443776 | bytes 6554112 | tf_op jit(solution)/shard_map/dot_general | solution.py:48
  83.8 2.1 fusion.18
  85.9 3.2 %convolution_convert_fusion = bf16[2048,1024]{1,0:T(8,128)(2,1)} fusion(bf16[2048,128]{1,0:T(8,128)(2,1)S(1)} %get-tuple-element.4, bf16[1024,128]{1,0:T(8,128)(2,1)S(1)} %copy-done), kind=kOutput, calls=%fused_computation.4 | convolution fusion | flops 538968064 | bytes 4980736 | tf_op jit(solution)/shard_map/dot_general | solution.py:58
  89.1 0.0 all-reduce.2.cloned.1.call-update
  89.1 0.0 reduce-scatter.5.cloned.1.call-start
  89.1 20.3 %reshape.34 = bf16[64,32,32,32]{3,2,1,0:T(8,128)(2,1)} reshape(bf16[2048,1024]{1,0:T(8,128)(2,1)} %convolution_convert_fusion) | data formatting | bytes 8388608 | tf_op jit(solution)/shard_map/reshape | solution.py:59
  109.5 11.0 %fusion.12 = f32[128,32,32]{0,2,1:T(8,128)S(1)} fusion(bf16[64,32,32,32]{3,2,1,0:T(8,128)(2,1)} %reshape.34, bf16[128,64,32,1]{2,1,0,3:T(8,128)(2,1)S(1)} %bitcast.42), kind=kOutput, calls=%fused_computation.12 | convolution fusion | flops 537001984 | bytes 5242880 | tf_op jit(solution)/shard_map/ijce,sic->sje/dot_general | solution.py:65
  120.5 1.0 copy.24
  121.5 0.0 reduce-scatter.5.cloned.1.call-update
  121.5 0.3 reduce-scatter.3.cloned.1.call-start
  121.8 9.2 %fusion.6 = f32[64,32,128]{2,1,0:T(8,128)S(1)} fusion(bf16[64,32,32,32]{3,2,1,0:T(8,128)(2,1)} %reshape.34, bf16[128,32,32,1]{0,2,1,3:T(8,128)(2,1)S(1)} %bitcast.44), kind=kOutput, calls=%fused_computation.10 | convolution fusion | flops 537133056 | bytes 5505024 | tf_op jit(solution)/shard_map/ijce,sje->sic/dot_general | solution.py:61
  131.1 1.3 copy.21
  132.4 0.0 reduce-scatter.3.cloned.1.call-update
  132.4 87.0 %all-reduce.2.cloned.1.call-done = f32[1024,128]{1,0:T(8,128)} async-done(((f32[1024,128]{1,0:T(8,128)}), f32[1024,128]{1,0:T(8,128)}) %all-reduce.2.cloned.1.call-update) | async-done | bytes 524304 | tf_op jit(solution)/shard_map/psum | solution.py:57
  219.4 1.9 copy.53
  (10 shorter events, 0.2 us)
Async XLA Ops:
  8.0 71.1 %copy-start = (bf16[1024,128]{1,0:T(8,128)(2,1)S(1)}, bf16[1024,128]{1,0:T(8,128)(2,1)}, u32[]{:S(2)}) copy-start(bf16[1024,128]{1,0:T(8,128)(2,1)} %param.7) | copy-start | bytes 786436
  8.0 211.4 %all-reduce.2.cloned.1.call-start = ((), (), s32[]{:S(2)}) async-start(), calls=%async_computation.4 | async-start | bytes 1048576 | tf_op jit(solution)/shard_map/psum | solution.py:57
  8.1 5.5 %collective-permute-start = (bf16[1,16,2048]{2,1,0:T(8,128)(2,1)}, bf16[1,16,2048]{2,1,0:T(8,128)(2,1)S(1)}, u32[]{:S(2)}, u32[]{:S(2)}) collective-permute-start(bf16[1,16,2048]{2,1,0:T(8,128)(2,1)} %bitcast.48), channel_id=1, source_target_pairs={{0,1},{1,0},{2,3},{3,2},{4,5},{5,4},{6,7},{7,6},{8,9},{9,8},{10,11... | collective-permute-start | bytes 196616 | tf_op jit(solution)/shard_map/ppermute | solution.py:22
  14.4 8.3 %collective-permute-start.1 = (bf16[2,16,2048]{2,1,0:T(8,128)(2,1)S(1)}, bf16[2,16,2048]{2,1,0:T(8,128)(2,1)S(1)}, u32[]{:S(2)}, u32[]{:S(2)}) collective-permute-start(bf16[2,16,2048]{2,1,0:T(8,128)(2,1)S(1)} %pad_maximum_fusion.2), channel_id=1, source_target_pairs={{0,2},{1,3},{2,0},{3,1},{4,6},{5,7},{6,4},{7,5},{8,10},{9,11},{10,... | collective-permute-start | bytes 393224 | tf_op jit(solution)/shard_map/ppermute | solution.py:22
  22.8 15.0 %collective-permute-start.2 = (bf16[4,16,2048]{2,1,0:T(8,128)(2,1)S(1)}, bf16[4,16,2048]{2,1,0:T(8,128)(2,1)S(1)}, u32[]{:S(2)}, u32[]{:S(2)}) collective-permute-start(bf16[4,16,2048]{2,1,0:T(8,128)(2,1)S(1)} %pad_maximum_fusion.1), channel_id=1, source_target_pairs={{0,4},{1,5},{2,6},{3,7},{4,0},{5,1},{6,2},{7,3},{8,12},{9,13},{10,... | collective-permute-start | bytes 786440 | tf_op jit(solution)/shard_map/ppermute | solution.py:22
  55.8 23.3 %copy-start.2 = (f32[128]{0:T(128)S(1)}, f32[128]{0:T(128)}, u32[]{:S(2)}) copy-start(f32[128]{0:T(128)} %param.8) | copy-start | bytes 1540
  79.1 4.7 %copy-start.1 = (bf16[2048,1024]{1,0:T(8,128)(2,1)S(1)}, bf16[2048,1024]{1,0:T(8,128)(2,1)}, u32[]{:S(2)}) copy-start(bf16[2048,1024]{1,0:T(8,128)(2,1)} %reshape.32) | copy-start | bytes 12582916
  89.1 130.3 %reduce-scatter.5.cloned.1.call-start = ((), (), s32[]{:S(2)}) async-start(), calls=%async_computation.3 | async-start | bytes 655360 | tf_op jit(solution)/shard_map/reduce_scatter | solution.py:70
  121.5 97.9 %reduce-scatter.3.cloned.1.call-start = ((), (), s32[]{:S(2)}) async-start(), calls=%async_computation.2 | async-start | bytes 1179648 | tf_op jit(solution)/shard_map/reduce_scatter | solution.py:67
Sparse Core Ops, SparseCore 0:
  89.2 130.1 all-reduce.1
Sparse Core Ops, SparseCore 1:
  121.6 21.9 reduce-scatter.4
  147.4 64.3 reduce-scatter.2
